TPU v7x, 256 devices: a whole 4x4x8 slice. The times are simulated.
256 devices in a mesh: expert: 32 (over y, z), vocab: 8 (over x, core).
Axes of the slice: x: 4, y: 4, z: 8, core: 2. Of those that a mesh axis runs over, the one named last changes fastest.
Arguments:
- layer_out: bfloat16 [1024, 2048], P('expert'), may hold values from -6 to 6
- moe_input: bfloat16 [1024, 2048], P('expert'), may hold values from -6 to 6
- final_gain: float32 [2048], replicated, may hold values from 0.1 to 1.9
- head_weight: bfloat16 [2048, 98304], P(None, ('expert', 'vocab')), may hold values from -0.125 to 0.125
- clean_ids: int32 [1024], P('expert'), may hold values from 0 to 98303
- levels: int32 [1024], P('expert'), may hold values from 0 to 15
- ratio_table: float32 [16], replicated, may hold values from 0.5 to 8
- gate_weights: float32 [1024, 8], P('expert'), may hold values from 0.05 to 0.5
- expert_ids: int32 [1024, 8], P('expert'), may hold values from 0 to 63, all different within a row; in each aligned block of 32 rows (0 to 31, 32 to 63, ...) at most 8 rows name the same one
- w_gate: bfloat16 [64, 2048, 1024], P('expert', None, 'vocab'), may hold values from -0.125 to 0.125
- w_up: bfloat16 [64, 2048, 1024], P('expert', None, 'vocab'), may hold values from -0.125 to 0.125
- w_down: bfloat16 [64, 1024, 2048], P('expert', 'vocab'), may hold values from -0.1875 to 0.1875
Outputs:
- head_grad: float32 [2048, 98304], P(None, ('expert', 'vocab'))
- residual_grad: float32 [1024, 2048], P('expert', 'vocab')
- input_grad: float32 [1024, 2048], P('expert', 'vocab')
Inputs may be any that keep to these rules, and one draw needn't show every extreme that they name: `expert_ids`: the 8 experts of a row are distinct; among the 32 rows of one index of expert no expert is named by more than 8 rows.
All inputs are finite; a program needn't handle non-finite values.
Results may differ from a plain program's by a relative error of at most 0.0044.
The roundings to bfloat16 on the way count: a program that leaves them out, or rounds other values in their place, can miss the bound.
Values may be sent and summed in bfloat16 or wider, within the bound.
No kernel may reach another device: no remote copies, remote signals or barrier semaphores. Data moves between devices by JAX's collectives and lax.ppermute only.
A program may use at most 64 MiB of HBM per device.

v0:
```python
import math
import jax
import jax.numpy as jnp
from jax import lax
from jax.sharding import PartitionSpec as P

epsilon = 1e-05


def sent_to_all(shard, axis):
    peers = lax.axis_size(axis)
    return lax.all_to_all(
        jnp.broadcast_to(shard[None], (peers, *shard.shape)), axis, 0, 0, tiled=True
    )


def of_everyone(shard, axis):
    everything = sent_to_all(shard, axis)
    return jnp.sum(everything, axis=0)


def sent_together(arrays, axis, split_dim, concat_dim, along):
    ends, at = ([], 0)
    for a in arrays[:-1]:
        at += a.shape[along]
        ends.append(at)
    both = jnp.concatenate(arrays, axis=along)
    return tuple(
        jnp.split(
            lax.all_to_all(both, axis, split_axis=split_dim, concat_axis=concat_dim, tiled=True),
            ends,
            axis=along,
        )
    )


def in_one_piece(arrays, axis, dim, along):
    widths = [a.shape[along] for a in arrays]
    both = jnp.concatenate(arrays, axis=along)
    result = lax.all_gather(both, axis, axis=dim, tiled=True)
    return tuple(jnp.split(result, [sum(widths[:k]) for k in range(1, len(widths))], axis=along))


def split_up(shard, dim, peers):
    before, after = (shard.shape[:dim], shard.shape[dim + 1 :])
    return jnp.moveaxis(shard.reshape(*before, peers, -1, *after), dim, 0)


def sum_at_owner(shard, axis, dim):
    parts = split_up(shard, dim, lax.axis_size(axis))
    arrived = lax.all_to_all(parts, axis, split_axis=0, concat_axis=0, tiled=True)
    return arrived.sum(axis=0)


def on_device(
    layer_out,
    moe_input,
    final_gain,
    head_weight,
    clean_ids,
    levels,
    ratio_table,
    gate_weights,
    expert_ids,
    w_gate,
    w_up,
    w_down,
):
    rows_local, model_width = layer_out.shape
    top_count = expert_ids.shape[1]
    n_expert = lax.axis_size("expert")
    n_vocab = lax.axis_size("vocab")
    total_rows = rows_local * n_expert
    local_experts = w_gate.shape[0]
    experts_all = local_experts * n_expert
    capacity = max(2, 2 * rows_local * top_count // experts_all)
    feature_share = model_width // n_vocab
    vocab_local = head_weight.shape[1]
    values = layer_out.astype(jnp.float32)
    row_scale = jnp.sqrt(jnp.mean(values * values, axis=1, keepdims=True) + epsilon)
    unit_rows = values / row_scale
    normed = (unit_rows * final_gain[None, :]).astype(jnp.bfloat16)
    normed_all, clean_all, level_all = (
        lax.all_gather(normed, "expert", axis=0, tiled=True),
        lax.all_gather(clean_ids, "expert", axis=0, tiled=True),
        lax.all_gather(levels, "expert", axis=0, tiled=True),
    )
    level_labels = jnp.arange(ratio_table.shape[0], dtype=jnp.int32)
    ratio_rows = jnp.sum(
        jnp.where(level_all[:, None] == level_labels[None, :], ratio_table[None, :], 0.0), axis=1
    )
    column_start = (lax.axis_index("expert") * n_vocab + lax.axis_index("vocab")) * vocab_local
    columns = column_start + jnp.arange(vocab_local, dtype=jnp.int32)
    scores = jnp.dot(normed_all, head_weight, preferred_element_type=jnp.float32)
    target_hit = (clean_all[:, None] == columns[None, :]).astype(jnp.float32)
    loss_scale = 1.0 / math.sqrt(total_rows)
    score_grad = ((jnp.exp(scores) - ratio_rows[:, None] * target_hit) * loss_scale).astype(
        jnp.bfloat16
    )
    head_grad = lax.dot_general(
        normed_all, score_grad, (((0,), (0,)), ((), ())), preferred_element_type=jnp.float32
    )
    partial_grad = lax.psum_scatter(
        lax.dot_general(
            score_grad, head_weight, (((1,), (1,)), ((), ())), preferred_element_type=jnp.float32
        ),
        "expert",
        scatter_dimension=0,
        tiled=True,
    )
    normed_grad = of_everyone(partial_grad, "vocab")
    gained = final_gain[None, :] * normed_grad
    residual_full = (
        gained - unit_rows * jnp.mean(unit_rows * gained, axis=1, keepdims=True)
    ) / row_scale
    feature_start = lax.axis_index("vocab") * feature_share
    residual_grad = lax.dynamic_slice_in_dim(residual_full, feature_start, feature_share, 1)
    flat_ids = expert_ids.reshape(-1)
    labels = jnp.arange(experts_all, dtype=jnp.int32)
    onehot = (flat_ids[:, None] == labels[None, :]).astype(jnp.int32)
    earlier = jnp.cumsum(onehot, axis=0) - onehot
    slot_index = jnp.sum(earlier * onehot, axis=1)
    position = flat_ids * capacity + slot_index
    routed_grad = (
        (gate_weights[:, :, None] * residual_full[:, None, :])
        .astype(jnp.bfloat16)
        .reshape(-1, model_width)
    )
    inputs_rep = jnp.repeat(moe_input, top_count, axis=0)
    buffer_rows = experts_all * capacity
    send_inputs = (
        jnp.zeros((buffer_rows, model_width), jnp.bfloat16)
        .at[position]
        .set(inputs_rep)
        .reshape(experts_all, capacity, model_width)
    )
    send_grads = (
        jnp.zeros((buffer_rows, model_width), jnp.bfloat16)
        .at[position]
        .set(routed_grad)
        .reshape(experts_all, capacity, model_width)
    )
    part_inputs = lax.dynamic_slice_in_dim(send_inputs, feature_start, feature_share, 2)
    part_grads = lax.dynamic_slice_in_dim(send_grads, feature_start, feature_share, 2)
    moved_inputs, moved_grads = sent_together((part_inputs, part_grads), "expert", 0, 1, 2)
    inputs_slot, grads_slot = in_one_piece((moved_inputs, moved_grads), "vocab", 2, 0)
    gate_pre = jnp.einsum("esd,edf->esf", inputs_slot, w_gate, preferred_element_type=jnp.float32)
    up_pre = jnp.einsum("esd,edf->esf", inputs_slot, w_up, preferred_element_type=jnp.float32)
    act_grad = jnp.einsum("esd,efd->esf", grads_slot, w_down, preferred_element_type=jnp.float32)
    sigmoid_gate = jax.nn.sigmoid(gate_pre)
    gate_grad = (act_grad * up_pre * sigmoid_gate * (1.0 + gate_pre * (1.0 - sigmoid_gate))).astype(
        jnp.bfloat16
    )
    up_grad = (act_grad * gate_pre * sigmoid_gate).astype(jnp.bfloat16)
    partial_input = jnp.einsum(
        "esf,edf->esd", gate_grad, w_gate, preferred_element_type=jnp.float32
    )
    partial_input = partial_input + jnp.einsum(
        "esf,edf->esd", up_grad, w_up, preferred_element_type=jnp.float32
    )
    slot_share = sum_at_owner(partial_input, "vocab", 2)
    returned = lax.all_to_all(slot_share, "expert", split_axis=1, concat_axis=0, tiled=True)
    per_pair = returned.reshape(-1, feature_share)[position]
    input_grad = jnp.sum(per_pair.reshape(rows_local, top_count, feature_share), axis=1)
    return (head_grad, residual_grad, input_grad)


def solution(mesh):
    in_specs = (
        P("expert", None),
        P("expert", None),
        P(),
        P(None, ("expert", "vocab")),
        P("expert"),
        P("expert"),
        P(),
        P("expert", None),
        P("expert", None),
        P("expert", None, "vocab"),
        P("expert", None, "vocab"),
        P("expert", "vocab", None),
    )
    out_specs = (P(None, ("expert", "vocab")), P("expert", "vocab"), P("expert", "vocab"))
    return jax.shard_map(
        on_device, mesh=mesh, in_specs=in_specs, out_specs=out_specs, check_vma=False
    )
```

profile of v0, /device:TPU:32, one launch (start us, length us, event | category | flops | bytes accessed | tf_op | source)
XLA Modules:
  0.0 536.3 jit_solution(17601662020850642282)
XLA Ops:
  7.2 1.1 fusion.27
  8.4 1.7 multiply_convert_fusion.4
  10.2 1.3 dynamic-slice
  13.8 23.3 %all-reduce.2 = (s32[1024]{0:T(1024)S(1)}, s32[1024]{0:T(1024)S(1)}) all-reduce(s32[1024]{0:T(1024)S(1)} %dynamic-update-slice.1, s32[1024]{0:T(1024)S(1)} %dynamic-update-slice), channel_id=1, replica_groups=mesh['expert'=32,'vocab'=8] {'expert'}, use_global_device_ids=true, to_apply=%add.1 | all-reduce | flops 2048 | bytes 16384
  37.8 58.0 %all-gather.3.cloned.1.call-done = bf16[1024,2048]{1,0:T(8,128)(2,1)} async-done(((bf16[32,2048]{1,0:T(8,128)(2,1)}), bf16[1024,2048]{1,0:T(8,128)(2,1)}) %all-gather.3.cloned.1.call-update) | async-done | bytes 4194320 | tf_op jit(solution)/shard_map/all_gather | solution.py:84
  95.8 4.5 fusion.39
  100.3 1.2 copy-done.4
  101.5 5.7 %fusion.1 = f32[1024,2048]{1,0:T(8,128)} fusion(bf16[2048,384]{1,0:T(8,128)(2,1)S(1)} %copy-done, f32[1024,384]{1,0:T(8,128)S(1)} %fusion.39, f32[1024]{0:T(1024)S(1)} %select_reduce_fusion, s32[384]{0:T(512)S(1)} %iota_add_fusion, s32[1024]{0:T(1024)S(1)} %get-tuple-element.4), kind=kOutput, calls=%fused_computation.8 | convolution fusion | flops 1612578816 | bytes 11544064 | tf_op jit(solution)/shard_map/dot_general | solution.py:104
  107.2 225.0 %reduce-scatter.2.cloned.1.call-done = f32[32,2048]{1,0:T(8,128)} async-done(((f32[1024,2048]{1,0:T(8,128)}), f32[32,2048]{1,0:T(8,128)}) %reduce-scatter.2.cloned.1.call-update) | async-done | bytes 262160 | tf_op jit(solution)/shard_map/reduce_scatter | solution.py:103
  332.2 2.5 broadcast_in_dim.18
  334.7 4.5 all-to-all-start
  340.9 3.7 scatter_custom_fusion
  344.6 21.8 %all-to-all-done = f32[8,32,2048]{2,1,0:T(8,128)} async-done(((f32[8,32,2048]{2,1,0:T(8,128)}), f32[8,32,2048]{2,1,0:T(8,128)}, u32[]{:S(2)}, u32[]{:S(2)}) %all-to-all-start) | async-done | bytes 2097184 | tf_op jit(solution)/shard_map/all_to_all | solution.py:12
  366.4 1.7 reduce_sum.67
  368.5 3.8 scatter_custom_fusion.1
  373.4 25.3 %all_to_all.43 = bf16[64,8,512]{2,1,0:T(8,128)(2,1)S(1)} all-to-all(bf16[64,8,512]{2,1,0:T(8,128)(2,1)S(1)} %pad_maximum_fusion), channel_id=1, replica_groups=mesh['expert'=32,'vocab'=8] {'expert'}, dimensions={0} | all-to-all | bytes 1048576 | tf_op jit(solution)/shard_map/all_to_all | solution.py:30
  399.7 33.0 %all-gather.5.cloned.1.call-done = bf16[4,256,2048]{2,1,0:T(8,128)(2,1)} async-done(((bf16[4,256,256]{2,1,0:T(8,128)(2,1)}), bf16[4,256,2048]{2,1,0:T(8,128)(2,1)}) %all-gather.5.cloned.1.call-update) | async-done | bytes 4194320 | tf_op jit(solution)/shard_map/all_gather | solution.py:40
  432.6 2.7 fusion.41
  439.6 54.2 %all_to_all.44 = f32[8,2,256,256]{3,2,1,0:T(8,128)} all-to-all(f32[8,2,256,256]{3,2,1,0:T(8,128)S(1)} %bitcast.67), channel_id=1, replica_groups=mesh['expert'=32,'vocab'=8] {'vocab'}, dimensions={0} | all-to-all | bytes 8388608 | tf_op jit(solution)/shard_map/all_to_all | solution.py:51
  493.8 3.3 reduce_sum.71
  497.1 2.4 copy.48
  499.5 10.1 %all-to-all-start.3 = ((f32[2,256,256]{2,0,1:T(2,128)}), f32[2,256,256]{2,0,1:T(2,128)}, u32[]{:S(2)}, u32[]{:S(2)}) async-start(f32[2,256,256]{2,0,1:T(2,128)} %copy.48), calls=%async_computation.4 | async-start | bytes 1048576 | tf_op jit(solution)/shard_map/all_to_all | solution.py:162
  509.7 6.3 %fusion.2 = f32[2048,384]{1,0:T(8,128)} fusion(bf16[1024,2048]{1,0:T(8,128)(2,1)} %all-gather.3.cloned.1.call-done, f32[1024,384]{1,0:T(8,128)S(1)} %copy-done.5, f32[1024]{0:T(1024)S(1)} %select_reduce_fusion, s32[384]{0:T(512)S(1)} %iota_add_fusion, s32[1024]{0:T(1024)S(1)} %get-tuple-element.4), kind=kOutput, calls=%fused_computation.9 | convolution fusion | flops 1612578816 | bytes 8922624 | tf_op jit(solution)/shard_map/dot_general | solution.py:100
  516.6 10.4 %all-to-all-done.3 = f32[2,256,256]{2,0,1:T(2,128)} async-done(((f32[2,256,256]{2,0,1:T(2,128)}), f32[2,256,256]{2,0,1:T(2,128)}, u32[]{:S(2)}, u32[]{:S(2)}) %all-to-all-start.3) | async-done | bytes 524320 | tf_op jit(solution)/shard_map/all_to_all | solution.py:162
  (68 shorter events, 14.2 us)
Async XLA Ops:
  7.2 88.7 %copy-start = (bf16[2048,384]{1,0:T(8,128)(2,1)S(1)}, bf16[2048,384]{1,0:T(8,128)(2,1)}, u32[]{:S(2)}) copy-start(bf16[2048,384]{1,0:T(8,128)(2,1)} %param.15) | copy-start | bytes 4718596
  7.2 88.6 %all-gather.3.cloned.1.call-start = ((), (), s32[]{:S(2)}) async-start(), calls=%async_computation.5 | async-start | bytes 4325376 | tf_op jit(solution)/shard_map/all_gather | solution.py:84
  10.1 322.1 %reduce-scatter.2.cloned.1.call-start = ((), (), s32[]{:S(2)}) async-start(), calls=%async_computation.6 | async-start | bytes 8650752 | tf_op jit(solution)/shard_map/reduce_scatter | solution.py:103
  100.3 1.2 copy-start.4
  334.7 4.5 copy-start.9
  334.7 5.8 %copy-start.10 = (f32[32,8]{0,1:T(8,128)S(1)}, f32[32,8]{0,1:T(8,128)}, u32[]{:S(2)}) copy-start(f32[32,8]{0,1:T(8,128)} %param.19) | copy-start | bytes 3076
  334.7 6.1 %copy-start.7 = (bf16[32,2048]{1,0:T(8,128)(2,1)S(1)}, bf16[32,2048]{1,0:T(8,128)(2,1)}, u32[]{:S(2)}) copy-start(bf16[32,2048]{1,0:T(8,128)(2,1)} %param.13) | copy-start | bytes 393220
  334.7 31.7 %all-to-all-start = ((f32[8,32,2048]{2,1,0:T(8,128)}), f32[8,32,2048]{2,1,0:T(8,128)}, u32[]{:S(2)}, u32[]{:S(2)}) async-start(f32[8,32,2048]{2,1,0:T(8,128)} %broadcast_in_dim.18), calls=%async_computation.1 | async-start | bytes 4194304 | tf_op jit(solution)/shard_map/all_to_all | solution.py:12
  339.2 93.4 %all-gather.5.cloned.1.call-start = ((), (), s32[]{:S(2)}) async-start(), calls=%async_computation.7 | async-start | bytes 4718592 | tf_op jit(solution)/shard_map/all_gather | solution.py:40
  340.8 27.3 %copy-start.6 = (bf16[32,2048]{1,0:T(8,128)(2,1)S(1)}, bf16[32,2048]{1,0:T(8,128)(2,1)}, u32[]{:S(2)}) copy-start(bf16[32,2048]{1,0:T(8,128)(2,1)} %param.12) | copy-start | bytes 393220
  340.9 27.3 %copy-start.8 = (f32[2048]{0:T(1024)S(1)}, f32[2048]{0:T(1024)}, u32[]{:S(2)}) copy-start(f32[2048]{0:T(1024)} %param.14) | copy-start | bytes 24580
  399.7 35.7 %copy-start.3 = (bf16[2,2048,128]{2,1,0:T(8,128)(2,1)S(1)}, bf16[2,2048,128]{2,1,0:T(8,128)(2,1)}, u32[]{:S(2)}) copy-start(bf16[2,2048,128]{2,1,0:T(8,128)(2,1)} %param.21) | copy-start | bytes 3145732
  432.6 3.1 copy-start.1
  435.8 1.2 copy-start.2
  497.1 12.5 %copy-start.5 = (f32[1024,384]{1,0:T(8,128)S(1)}, f32[1024,384]{1,0:T(8,128)}, u32[]{:S(2)}) copy-start(f32[1024,384]{1,0:T(8,128)} %copy-done.4) | copy-start | bytes 4718596
  499.5 27.5 %all-to-all-start.3 = ((f32[2,256,256]{2,0,1:T(2,128)}), f32[2,256,256]{2,0,1:T(2,128)}, u32[]{:S(2)}, u32[]{:S(2)}) async-start(f32[2,256,256]{2,0,1:T(2,128)} %copy.48), calls=%async_computation.4 | async-start | bytes 1048576 | tf_op jit(solution)/shard_map/all_to_all | solution.py:162
Sparse Core Ops, SparseCore 0:
  11.2 84.6 all-gather.2
  107.3 224.8 reduce-scatter.1
  399.8 32.8 all-gather.4
where the time goes:
time: 537 us; the launch traced here: 536 us
  waiting for transfers between devices  348 us (65%)
  blocking collectives  103 us (19%)
  matrix products  22 us (4%)
  local copies, waits for them, and re-layouts  18.8 us (4%)
  other arithmetic  15.1 us (3%)
  starting transfers between devices  14.7 us (3%)
  between operations  14.7 us (3%)
    reduce_scatter x1, waiting for transfers between devices, on_device(): lax.psum_scatter(lax.dot_general(score_grad, head_weight, (((1,), (1,)),...  225 us
    all_gather x1, waiting for transfers between devices, on_device(): lax.all_gather(normed, 'expert', axis=0, tiled=True)  58 us
    all_to_all x1, blocking collectives, sum_at_owner(): lax.all_to_all(parts, axis, split_axis=0, concat_axis=0, tiled=True)  54.2 us
    all_gather x1, waiting for transfers between devices, in_one_piece(): result = lax.all_gather(both, axis, axis=dim, tiled=True)  33 us
    all_to_all x1, blocking collectives, sent_together(): lax.all_to_all(both, axis, split_axis=split_dim, concat_axis=concat_dim,...  25.3 us
    unnamed x1, blocking collectives  23.3 us
    all_to_all x1, waiting for transfers between devices, sent_to_all(): lax.all_to_all(jnp.broadcast_to(shard[None], (peers, *shard.shape)), axis...  21.8 us
  transfers between devices with their start and end apart: 5, of which 5 were waited for; matrix products, arithmetic and copies ran while one was open for 3% of the time, Pallas kernels for 0%

commit v1 on v0

--- a/solution.py
+++ b/solution.py
@@ -81,7 +81,9 @@
     unit_rows = values / row_scale
     normed = (unit_rows * final_gain[None, :]).astype(jnp.bfloat16)
     normed_all, clean_all, level_all = (
-        lax.all_gather(normed, "expert", axis=0, tiled=True),
+        jnp.concatenate(
+            lax.all_to_all(jnp.stack([normed] * lax.axis_size("expert")), "expert", 0, 0), axis=0
+        ),
         lax.all_gather(clean_ids, "expert", axis=0, tiled=True),
         lax.all_gather(levels, "expert", axis=0, tiled=True),
     )

time: 537 us -> 573 us (1.067)
  blocking collectives: 103 us -> 183 us
  waiting for transfers between devices: 348 us -> 293 us
  starting transfers between devices: 14.7 us -> 26.3 us
    unnamed x1, blocking collectives: 23.3 us -> 104 us
    all_gather x1 -> x0, waiting for transfers between devices: 58 us -> none  [on_device(): lax.all_gather(normed, 'expert', axis=0, tiled=True)]
    all_to_all x0 -> x1, starting transfers between devices: none -> 11.6 us  [on_device(): lax.all_to_all(jnp.stack([normed] * lax.axis_size('expert')), 'expert', 0...]
  transfers between devices with their start and end apart: 5 -> 5, of which waited for: 5 -> 4; matrix products, arithmetic and copies ran while one was open for 3% -> 2% of each run, Pallas kernels for 0% -> 0%
where the time goes in v1:
time: 573 us; the launch traced here: 572 us
  waiting for transfers between devices  293 us (51%)
  blocking collectives  183 us (32%)
  starting transfers between devices  26.3 us (5%)
  matrix products  22 us (4%)
  local copies, waits for them, and re-layouts  19.3 us (3%)
  between operations  15 us (3%)
  other arithmetic  13.8 us (2%)
    reduce_scatter x1, waiting for transfers between devices, on_device(): lax.psum_scatter(lax.dot_general(score_grad, head_weight, (((1,), (1,)),...  227 us
    unnamed x1, blocking collectives  104 us
    all_to_all x1, blocking collectives, sum_at_owner(): lax.all_to_all(parts, axis, split_axis=0, concat_axis=0, tiled=True)  54.2 us
    all_gather x1, waiting for transfers between devices, in_one_piece(): result = lax.all_gather(both, axis, axis=dim, tiled=True)  33 us
    all_to_all x1, blocking collectives, sent_together(): lax.all_to_all(both, axis, split_axis=split_dim, concat_axis=concat_dim,...  25.3 us
    all_to_all x1, waiting for transfers between devices, sent_to_all(): lax.all_to_all(jnp.broadcast_to(shard[None], (peers, *shard.shape)), axis...  21.8 us
    all_to_all x1, starting transfers between devices, on_device(): lax.all_to_all(jnp.stack([normed] * lax.axis_size('expert')), 'expert', 0...  11.6 us
  transfers between devices with their start and end apart: 5, of which 4 were waited for; matrix products, arithmetic and copies ran while one was open for 2% of the time, Pallas kernels for 0%

profile of v1, /device:TPU:32, one launch (start us, length us, event | category | flops | bytes accessed | tf_op | source)
XLA Modules:
  0.0 572.4 jit_solution(7072301570850568783)
XLA Ops:
  7.2 1.2 fusion.27
  9.4 2.5 stack.2
  11.8 11.6 %all-to-all-start = ((bf16[32,32,2048]{2,1,0:T(8,128)(2,1)}), bf16[32,32,2048]{2,1,0:T(8,128)(2,1)}, u32[]{:S(2)}, u32[]{:S(2)}) async-start(bf16[32,32,2048]{2,1,0:T(8,128)(2,1)} %stack.2), calls=%async_computation | async-start | bytes 8388608 | tf_op jit(solution)/shard_map/all_to_all | solution.py:85
  25.2 103.9 %all-reduce.2 = (s32[1024]{0:T(1024)S(1)}, s32[1024]{0:T(1024)S(1)}) all-reduce(s32[1024]{0:T(1024)S(1)} %dynamic-update-slice.1, s32[1024]{0:T(1024)S(1)} %dynamic-update-slice), channel_id=1, replica_groups=mesh['expert'=32,'vocab'=8] {'expert'}, use_global_device_ids=true, to_apply=%add.1 | all-reduce | flops 2048 | bytes 16384
  129.3 4.5 fusion.39
  133.8 1.2 copy-done.4
  135.0 5.7 fusion.1
  140.6 227.5 %reduce-scatter.2.cloned.1.call-done = f32[32,2048]{1,0:T(8,128)} async-done(((f32[1024,2048]{1,0:T(8,128)}), f32[32,2048]{1,0:T(8,128)}) %reduce-scatter.2.cloned.1.call-update) | async-done | bytes 262160 | tf_op jit(solution)/shard_map/reduce_scatter | solution.py:105
  368.1 2.5 broadcast_in_dim.18
  370.6 4.5 all-to-all-start.1
  376.8 3.7 scatter_custom_fusion
  380.5 21.8 %all-to-all-done.1 = f32[8,32,2048]{2,1,0:T(8,128)} async-done(((f32[8,32,2048]{2,1,0:T(8,128)}), f32[8,32,2048]{2,1,0:T(8,128)}, u32[]{:S(2)}, u32[]{:S(2)}) %all-to-all-start.1) | async-done | bytes 2097184 | tf_op jit(solution)/shard_map/all_to_all | solution.py:12
  402.3 1.7 reduce_sum.67
  404.4 3.8 scatter_custom_fusion.1
  409.3 25.3 %all_to_all.48 = bf16[64,8,512]{2,1,0:T(8,128)(2,1)S(1)} all-to-all(bf16[64,8,512]{2,1,0:T(8,128)(2,1)S(1)} %pad_maximum_fusion), channel_id=1, replica_groups=mesh['expert'=32,'vocab'=8] {'expert'}, dimensions={0} | all-to-all | bytes 1048576 | tf_op jit(solution)/shard_map/all_to_all | solution.py:30
  435.5 33.0 %all-gather.2.cloned.1.call-done = bf16[4,256,2048]{2,1,0:T(8,128)(2,1)} async-done(((bf16[4,256,256]{2,1,0:T(8,128)(2,1)}), bf16[4,256,2048]{2,1,0:T(8,128)(2,1)}) %all-gather.2.cloned.1.call-update) | async-done | bytes 4194320 | tf_op jit(solution)/shard_map/all_gather | solution.py:40
  468.5 2.7 fusion.41
  475.4 54.2 %all_to_all.49 = f32[8,2,256,256]{3,2,1,0:T(8,128)} all-to-all(f32[8,2,256,256]{3,2,1,0:T(8,128)S(1)} %bitcast.68), channel_id=1, replica_groups=mesh['expert'=32,'vocab'=8] {'vocab'}, dimensions={0} | all-to-all | bytes 8388608 | tf_op jit(solution)/shard_map/all_to_all | solution.py:51
  529.7 3.3 reduce_sum.71
  533.0 2.4 copy.48
  535.3 10.1 %all-to-all-start.4 = ((f32[2,256,256]{2,0,1:T(2,128)}), f32[2,256,256]{2,0,1:T(2,128)}, u32[]{:S(2)}, u32[]{:S(2)}) async-start(f32[2,256,256]{2,0,1:T(2,128)} %copy.48), calls=%async_computation.5 | async-start | bytes 1048576 | tf_op jit(solution)/shard_map/all_to_all | solution.py:164
  545.5 6.3 %fusion.2 = f32[2048,384]{1,0:T(8,128)} fusion(bf16[1024,2048]{1,0:T(8,128)(2,1)} %bitcast, f32[1024,384]{1,0:T(8,128)S(1)} %copy-done.5, f32[1024]{0:T(1024)S(1)} %select_reduce_fusion, s32[384]{0:T(512)S(1)} %iota_add_fusion, s32[1024]{0:T(1024)S(1)} %get-tuple-element.4), kind=kOutput, calls=%fused_computation.9 | convolution fusion | flops 1612578816 | bytes 8922624 | tf_op jit(solution)/shard_map/dot_general | solution.py:102
  552.5 10.4 %all-to-all-done.4 = f32[2,256,256]{2,0,1:T(2,128)} async-done(((f32[2,256,256]{2,0,1:T(2,128)}), f32[2,256,256]{2,0,1:T(2,128)}, u32[]{:S(2)}, u32[]{:S(2)}) %all-to-all-start.4) | async-done | bytes 524320 | tf_op jit(solution)/shard_map/all_to_all | solution.py:164
  562.8 1.1 copy.58
  (76 shorter events, 12.8 us)
Async XLA Ops:
  7.2 122.1 %copy-start = (bf16[2048,384]{1,0:T(8,128)(2,1)S(1)}, bf16[2048,384]{1,0:T(8,128)(2,1)}, u32[]{:S(2)}) copy-start(bf16[2048,384]{1,0:T(8,128)(2,1)} %param.15) | copy-start | bytes 4718596
  11.8 11.6 %copy-start.14 = (u32[256]{0:T(256)S(1)}, u32[256]{0:T(256)}, u32[]{:S(2)}) copy-start(u32[256]{0:T(256)} %constant.48) | copy-start | bytes 3076
  11.8 12.9 %copy-start.12 = (s32[32]{0:T(128)S(1)}, s32[32]{0:T(128)}, u32[]{:S(2)}) copy-start(s32[32]{0:T(128)} %param.17) | copy-start | bytes 388
  11.8 13.1 %copy-start.13 = (s32[32]{0:T(128)S(1)}, s32[32]{0:T(128)}, u32[]{:S(2)}) copy-start(s32[32]{0:T(128)} %param.16) | copy-start | bytes 388
  11.8 117.3 %copy-start.11 = (f32[16]{0:T(128)S(1)}, f32[16]{0:T(128)}, u32[]{:S(2)}) copy-start(f32[16]{0:T(128)} %param.18) | copy-start | bytes 196
  11.8 117.4 %all-to-all-start = ((bf16[32,32,2048]{2,1,0:T(8,128)(2,1)}), bf16[32,32,2048]{2,1,0:T(8,128)(2,1)}, u32[]{:S(2)}, u32[]{:S(2)}) async-start(bf16[32,32,2048]{2,1,0:T(8,128)(2,1)} %stack.2), calls=%async_computation | async-start | bytes 8388608 | tf_op jit(solution)/shard_map/all_to_all | solution.py:85
  23.4 344.7 %reduce-scatter.2.cloned.1.call-start = ((), (), s32[]{:S(2)}) async-start(), calls=%async_computation.6 | async-start | bytes 8650752 | tf_op jit(solution)/shard_map/reduce_scatter | solution.py:105
  133.8 1.2 copy-start.4
  370.6 4.5 copy-start.9
  370.6 5.8 %copy-start.10 = (f32[32,8]{0,1:T(8,128)S(1)}, f32[32,8]{0,1:T(8,128)}, u32[]{:S(2)}) copy-start(f32[32,8]{0,1:T(8,128)} %param.19) | copy-start | bytes 3076
  370.6 6.1 %copy-start.7 = (bf16[32,2048]{1,0:T(8,128)(2,1)S(1)}, bf16[32,2048]{1,0:T(8,128)(2,1)}, u32[]{:S(2)}) copy-start(bf16[32,2048]{1,0:T(8,128)(2,1)} %param.13) | copy-start | bytes 393220
  370.6 31.7 %all-to-all-start.1 = ((f32[8,32,2048]{2,1,0:T(8,128)}), f32[8,32,2048]{2,1,0:T(8,128)}, u32[]{:S(2)}, u32[]{:S(2)}) async-start(f32[8,32,2048]{2,1,0:T(8,128)} %broadcast_in_dim.18), calls=%async_computation.2 | async-start | bytes 4194304 | tf_op jit(solution)/shard_map/all_to_all | solution.py:12
  375.1 93.4 %all-gather.2.cloned.1.call-start = ((), (), s32[]{:S(2)}) async-start(), calls=%async_computation.7 | async-start | bytes 4718592 | tf_op jit(solution)/shard_map/all_gather | solution.py:40
  376.7 27.3 %copy-start.6 = (bf16[32,2048]{1,0:T(8,128)(2,1)S(1)}, bf16[32,2048]{1,0:T(8,128)(2,1)}, u32[]{:S(2)}) copy-start(bf16[32,2048]{1,0:T(8,128)(2,1)} %param.12) | copy-start | bytes 393220
  376.8 27.3 %copy-start.8 = (f32[2048]{0:T(1024)S(1)}, f32[2048]{0:T(1024)}, u32[]{:S(2)}) copy-start(f32[2048]{0:T(1024)} %param.14) | copy-start | bytes 24580
  435.5 35.7 %copy-start.3 = (bf16[2,2048,128]{2,1,0:T(8,128)(2,1)S(1)}, bf16[2,2048,128]{2,1,0:T(8,128)(2,1)}, u32[]{:S(2)}) copy-start(bf16[2,2048,128]{2,1,0:T(8,128)(2,1)} %param.21) | copy-start | bytes 3145732
  468.5 3.1 copy-start.1
  471.6 1.2 copy-start.2
  533.0 12.5 %copy-start.5 = (f32[1024,384]{1,0:T(8,128)S(1)}, f32[1024,384]{1,0:T(8,128)}, u32[]{:S(2)}) copy-start(f32[1024,384]{1,0:T(8,128)} %copy-done.4) | copy-start | bytes 4718596
  535.3 27.5 %all-to-all-start.4 = ((f32[2,256,256]{2,0,1:T(2,128)}), f32[2,256,256]{2,0,1:T(2,128)}, u32[]{:S(2)}, u32[]{:S(2)}) async-start(f32[2,256,256]{2,0,1:T(2,128)} %copy.48), calls=%async_computation.5 | async-start | bytes 1048576 | tf_op jit(solution)/shard_map/all_to_all | solution.py:164
Sparse Core Ops, SparseCore 0:
  140.8 227.2 reduce-scatter.1
  435.6 32.7 all-gather.1
